TPU v7x, 32 devices: a whole 2x2x4 slice. The times are simulated.
32 devices in a mesh: groups: 2 (over y), seq: 4 (over z), head: 4 (over x, core).
Axes of the slice: x: 2, y: 2, z: 4, core: 2. Of those that a mesh axis runs over, the one named last changes fastest.
Arguments:
- query: bfloat16 [8192, 1536], P(('groups', 'seq', 'head')), parts along dimension 0, may hold values from -150 to 150
- key_in: bfloat16 [8192, 1536], P(('groups', 'seq', 'head')), parts along dimension 0, may hold values from -6 to 6
- value: bfloat16 [8192, 1536], P(('groups', 'seq', 'head')), parts along dimension 0, may hold values from -6 to 6
- grad_out: bfloat16 [8192, 1536], P(('groups', 'seq', 'head')), parts along dimension 0, may hold values from -6 to 6
- pattern: int32 [16, 3], replicated, may hold values from 0 to 15, as said below
- live: int32 [16, 3], replicated, may hold values from 0 to 1, as said below
Outputs:
- attended: bfloat16 [8192, 1536], P(('groups', 'seq', 'head')), parts along dimension 0
- query_grad: bfloat16 [8192, 1536], P(('groups', 'seq', 'head')), parts along dimension 0
- key_grad: bfloat16 [8192, 1536], P(('groups', 'seq', 'head')), parts along dimension 0
- value_grad: bfloat16 [8192, 1536], P(('groups', 'seq', 'head')), parts along dimension 0
There are 2 independent parts, one for each index of `groups`. A program takes and returns all parts, laid end to end along the dimension named above; an argument that names none is the same for every part. Nothing has to cross between parts.
Inputs may be any that keep to these rules, and one draw needn't show every extreme that they name: `pattern`: each entry names a tile of the same frame-tile layer as its query tile or of the layer just before or after it; the live entries of a row are distinct; an entry that is not live names the query tile itself. Slot 0 of every row is live and names the query tile itself.
All inputs are finite; a program needn't handle non-finite values.
Results may differ from a plain program's by a relative error of at most 0.015.
Values may be sent and summed in bfloat16 or wider, within the bound.
A program may use at most 128 MiB of HBM per device.

v0:
```python
import jax
import jax.numpy as jnp
from jax import lax
from jax.sharding import PartitionSpec as P

HEADS = 12
HEAD_DIM = 128


def extended_2(cells, sides, width):
    for axis, dim in sides:
        count = lax.axis_size(axis)
        ends = count - 1
        head = lax.slice_in_dim(cells, 0, width, axis=dim)
        tail = lax.slice_in_dim(cells, cells.shape[dim] - width, cells.shape[dim], axis=dim)
        cells = jnp.concatenate(
            [
                lax.ppermute(tail, axis, [(i, (i + 1) % count) for i in range(ends)]),
                cells,
                lax.ppermute(head, axis, [((i + 1) % count, i) for i in range(ends)]),
            ],
            axis=dim,
        )
    return cells


def shifted(value, axis, steps):
    count = lax.axis_size(axis)
    initial, last = (max(0, -steps), min(count, count - steps))
    return lax.ppermute(value, axis, [(source, source + steps) for source in range(initial, last)])


def head_split(rows_flat, tiles, heads):
    width = rows_flat.shape[1]
    return rows_flat.reshape(tiles, rows_flat.shape[0] // tiles, heads, width // heads).transpose(
        2, 0, 1, 3
    )


def head_join(blocks):
    heads, tiles, tile_size, head_size = blocks.shape
    return blocks.transpose(1, 2, 0, 3).reshape(tiles * tile_size, heads * head_size)


def forward_head(q_tile, g_tile, k_all, v_all, tile_ids, alive, scale):
    k_sel = k_all[tile_ids]
    v_sel = v_all[tile_ids]
    scores = jnp.einsum("aqd,ankd->aqnk", q_tile, k_sel, preferred_element_type=jnp.float32) * scale
    scores = jnp.where(alive[:, None, :, None], scores, -jnp.inf)
    peak = jnp.max(scores, axis=(2, 3), keepdims=True)
    exponent = jnp.exp(scores - peak)
    total = jnp.sum(exponent, axis=(2, 3), keepdims=True)
    weights = exponent / total
    weights_low = weights.astype(jnp.bfloat16)
    attended = jnp.einsum(
        "aqnk,ankd->aqd", weights_low, v_sel, preferred_element_type=jnp.float32
    ).astype(jnp.bfloat16)
    weight_grad = jnp.einsum("aqd,ankd->aqnk", g_tile, v_sel, preferred_element_type=jnp.float32)
    delta = jnp.sum(weights * weight_grad, axis=(2, 3), keepdims=True)
    score_grad = (weights * (weight_grad - delta) * scale).astype(jnp.bfloat16)
    query_grad = jnp.einsum(
        "aqnk,ankd->aqd", score_grad, k_sel, preferred_element_type=jnp.float32
    ).astype(jnp.bfloat16)
    onehot = (
        tile_ids[:, :, None] == jnp.arange(k_all.shape[0], dtype=jnp.int32)[None, None, :]
    ).astype(jnp.float32)
    key_slots = jnp.einsum("aqnk,aqd->ankd", score_grad, q_tile, preferred_element_type=jnp.float32)
    value_slots = jnp.einsum(
        "aqnk,aqd->ankd", weights_low, g_tile, preferred_element_type=jnp.float32
    )
    key_sums = jnp.einsum("anj,ankd->jkd", onehot, key_slots, precision=lax.Precision.HIGHEST)
    value_sums = jnp.einsum("anj,ankd->jkd", onehot, value_slots, precision=lax.Precision.HIGHEST)
    return (attended, query_grad, key_sums, value_sums)


def body(query, key_in, value, grad_out, pattern, live):
    members = lax.axis_size("head")
    heads = HEADS // members
    scale = HEAD_DIM ** (-0.5)
    queries, keys, values, out_grads = (
        lax.all_to_all(query, "head", split_axis=1, concat_axis=0, tiled=True),
        lax.all_to_all(key_in, "head", split_axis=1, concat_axis=0, tiled=True),
        lax.all_to_all(value, "head", split_axis=1, concat_axis=0, tiled=True),
        lax.all_to_all(grad_out, "head", split_axis=1, concat_axis=0, tiled=True),
    )
    tile_size = queries.shape[0] // members
    margin = members * tile_size
    seq_index = lax.axis_index("seq")
    first = seq_index * members
    extended = extended_2(jnp.stack([keys, values]), (("seq", 1),), margin)
    rows = lax.dynamic_slice_in_dim(pattern, first, members, 0)
    alive_rows = lax.dynamic_slice_in_dim(live, first, members, 0)
    tile_ids = rows - first + members
    alive = alive_rows > 0
    q_heads = head_split(queries, members, heads)
    g_heads = head_split(out_grads, members, heads)
    k_heads = head_split(extended[0], 3 * members, heads)
    v_heads = head_split(extended[1], 3 * members, heads)

    def with_partials(operands):
        return forward_head(
            operands[0], operands[1], operands[2], operands[3], tile_ids, alive, scale
        )

    attended, query_grad, key_sums, value_sums = lax.map(
        with_partials, (q_heads, g_heads, k_heads, v_heads)
    )
    grads = jnp.stack([head_join(key_sums), head_join(value_sums)])
    from_above = shifted(grads[:, :margin].astype(jnp.bfloat16), "seq", -1).astype(jnp.float32)
    from_below = shifted(grads[:, 2 * margin :].astype(jnp.bfloat16), "seq", 1).astype(jnp.float32)
    owned = grads[:, margin : 2 * margin] + from_above + from_below
    key_own = owned[0]
    value_own = owned[1]
    result = (
        lax.all_to_all(head_join(attended), "head", split_axis=0, concat_axis=1, tiled=True),
        lax.all_to_all(head_join(query_grad), "head", split_axis=0, concat_axis=1, tiled=True),
        lax.all_to_all(
            key_own.astype(jnp.bfloat16), "head", split_axis=0, concat_axis=1, tiled=True
        ),
        lax.all_to_all(
            value_own.astype(jnp.bfloat16), "head", split_axis=0, concat_axis=1, tiled=True
        ),
    )
    return (result[0], result[1], result[2], result[3])


def solution(mesh):
    placed = (
        P(("groups", "seq", "head"), None),
        P(("groups", "seq", "head"), None),
        P(("groups", "seq", "head"), None),
        P(("groups", "seq", "head"), None),
        P(),
        P(),
    )
    return jax.shard_map(
        body,
        mesh=mesh,
        in_specs=placed,
        out_specs=(
            P(("groups", "seq", "head"), None),
            P(("groups", "seq", "head"), None),
            P(("groups", "seq", "head"), None),
            P(("groups", "seq", "head"), None),
        ),
        check_vma=False,
    )
```

profile of v0, /device:TPU:24, one launch (start us, length us, event | category | flops | bytes accessed | tf_op | source)
XLA Modules:
  0.0 323.6 jit_solution(741371311791878829)
XLA Ops:
  0.6 2.4 copy.43
  3.0 3.5 %all-to-all-start.1 = ((bf16[256,4,384]{0,2,1:T(8,128)(2,1)}), bf16[256,4,384]{0,2,1:T(8,128)(2,1)S(1)}, u32[]{:S(2)}, u32[]{:S(2)}) async-start(bf16[256,4,384]{0,2,1:T(8,128)(2,1)} %bitcast.30), calls=%async_computation.1 | async-start | bytes 1572864 | tf_op jit(solution)/shard_map/all_to_all | solution.py:82
  7.7 10.5 %all-to-all-done.1 = bf16[256,4,384]{0,2,1:T(8,128)(2,1)S(1)} async-done(((bf16[256,4,384]{0,2,1:T(8,128)(2,1)}), bf16[256,4,384]{0,2,1:T(8,128)(2,1)S(1)}, u32[]{:S(2)}, u32[]{:S(2)}) %all-to-all-start.1) | async-done | bytes 786464 | tf_op jit(solution)/shard_map/all_to_all | solution.py:82
  18.1 3.5 %all-to-all-start.2 = ((bf16[256,4,384]{0,2,1:T(8,128)(2,1)}), bf16[256,4,384]{0,2,1:T(8,128)(2,1)S(1)}, u32[]{:S(2)}, u32[]{:S(2)}) async-start(bf16[256,4,384]{0,2,1:T(8,128)(2,1)} %bitcast.33), calls=%async_computation.2 | async-start | bytes 1572864 | tf_op jit(solution)/shard_map/all_to_all | solution.py:83
  22.0 11.2 %all-to-all-done.2 = bf16[256,4,384]{0,2,1:T(8,128)(2,1)S(1)} async-done(((bf16[256,4,384]{0,2,1:T(8,128)(2,1)}), bf16[256,4,384]{0,2,1:T(8,128)(2,1)S(1)}, u32[]{:S(2)}, u32[]{:S(2)}) %all-to-all-start.2) | async-done | bytes 786464 | tf_op jit(solution)/shard_map/all_to_all | solution.py:83
  35.0 3.5 %collective-permute-start.1 = (bf16[2,1024,384]{2,1,0:T(8,128)(2,1)}, bf16[2,1024,384]{2,1,0:T(8,128)(2,1)}, u32[]{:S(2)}, u32[]{:S(2)}) collective-permute-start(bf16[2,1024,384]{2,1,0:T(8,128)(2,1)} %pad_maximum_fusion.1), channel_id=1, source_target_pairs={{4,0},{8,4},{12,8},{5,1},{9,5},{13,9},{6,2},{10,6},{14,10},{7,3},{... | collective-permute-start | bytes 4718600 | tf_op jit(solution)/shard_map/ppermute | solution.py:20
  40.9 3.5 %all-to-all-start = ((bf16[256,4,384]{0,2,1:T(8,128)(2,1)}), bf16[256,4,384]{0,2,1:T(8,128)(2,1)S(1)}, u32[]{:S(2)}, u32[]{:S(2)}) async-start(bf16[256,4,384]{0,2,1:T(8,128)(2,1)} %bitcast.26), calls=%async_computation | async-start | bytes 1572864 | tf_op jit(solution)/shard_map/all_to_all | solution.py:81
  45.9 25.2 %collective-permute-done.1 = bf16[2,1024,384]{2,1,0:T(8,128)(2,1)} collective-permute-done((bf16[2,1024,384]{2,1,0:T(8,128)(2,1)}, bf16[2,1024,384]{2,1,0:T(8,128)(2,1)}, u32[]{:S(2)}, u32[]{:S(2)}) %collective-permute-start.1) | collective-permute-done | bytes 1572896 | tf_op jit(solution)/shard_map/ppermute | solution.py:20
  71.1 5.2 %collective-permute-done = bf16[2,1024,384]{2,1,0:T(8,128)(2,1)} collective-permute-done((bf16[2,1024,384]{2,1,0:T(8,128)(2,1)}, bf16[2,1024,384]{2,1,0:T(8,128)(2,1)}, u32[]{:S(2)}, u32[]{:S(2)}) %collective-permute-start) | collective-permute-done | bytes 1572896 | tf_op jit(solution)/shard_map/ppermute | solution.py:18
  76.3 4.6 %pad_maximum_fusion = bf16[2,3072,384]{2,1,0:T(8,128)(2,1)} fusion(bf16[2,1024,384]{2,1,0:T(8,128)(2,1)} %collective-permute-done.1, bf16[1,1024,384]{2,1,0:T(8,128)(2,1)S(1)} %bitcast.172, bf16[1,1024,384]{2,1,0:T(8,128)(2,1)S(1)} %bitcast.170, bf16[2,1024,384]{2,1,0:T(8,128)(2,1)} %collective-permute-done), kind=kLoop, calls=%fused_computation.47 | loop fusion | flops 18874368 | bytes 9437184 | tf_op jit(solution)/shard_map/concatenate | solution.py:16
  81.0 4.2 %all-to-all-start.3 = ((bf16[256,4,384]{0,2,1:T(8,128)(2,1)}), bf16[256,4,384]{0,2,1:T(8,128)(2,1)}, u32[]{:S(2)}, u32[]{:S(2)}) async-start(bf16[256,4,384]{0,2,1:T(8,128)(2,1)} %bitcast.38), calls=%async_computation.3 | async-start | bytes 1572864 | tf_op jit(solution)/shard_map/all_to_all | solution.py:84
  85.2 4.3 %fusion.37 = (bf16[1,3072,384]{2,1,0:T(8,128)(2,1)}, bf16[1,3072,384]{2,1,0:T(8,128)(2,1)S(1)}) fusion(bf16[2,3072,384]{2,1,0:T(8,128)(2,1)} %pad_maximum_fusion), kind=kLoop, calls=%fused_computation.59 | loop fusion | bytes 9437184 | tf_op jit(solution)/shard_map/slice | solution.py:98
  89.4 4.3 %copy.49 = bf16[1,3072,384]{1,2,0:T(8,128)(2,1)} copy(bf16[1,3072,384]{2,1,0:T(8,128)(2,1)} %get-tuple-element.128) | data formatting | bytes 4718592 | tf_op jit(solution)/shard_map/slice | solution.py:98
  93.7 5.4 %reshape_squeeze.7 = bf16[12,256,3,128]{1,0,3,2:T(8,128)(2,1)} reshape(bf16[1,3072,384]{1,2,0:T(8,128)(2,1)} %copy.49) | data formatting | bytes 4718592 | tf_op jit(solution)/shard_map/reshape;squeeze | solution.py:35
  99.1 4.8 %copy.53 = bf16[3,12,256,128]{3,2,1,0:T(8,128)(2,1)} copy(bf16[3,12,256,128]{2,1,3,0:T(8,128)(2,1)} %bitcast.167) | data formatting | bytes 4718592 | tf_op jit(solution)/shard_map/while | solution.py:105
  103.9 2.7 copy.47
  106.6 5.4 %reshape_squeeze.6 = bf16[12,256,3,128]{1,0,3,2:T(8,128)(2,1)} reshape(bf16[1,3072,384]{1,2,0:T(8,128)(2,1)} %copy.47) | data formatting | bytes 4718592 | tf_op jit(solution)/shard_map/reshape;squeeze | solution.py:35
  112.0 4.8 %copy.52 = bf16[3,12,256,128]{3,2,1,0:T(8,128)(2,1)} copy(bf16[3,12,256,128]{2,1,3,0:T(8,128)(2,1)} %bitcast.168) | data formatting | bytes 4718592 | tf_op jit(solution)/shard_map/while | solution.py:105
  116.8 92.5 %while.16 = (s32[]{:T(128)}, bf16[3,4,256,128]{2,3,0,1:T(8,128)(2,1)}, bf16[3,4,256,128]{2,3,0,1:T(8,128)(2,1)}, f32[3,12,256,128]{3,1,2,0:T(8,128)}, f32[3,12,2...) while((s32[]{:T(128)}, ...), condition=%wide.region_4.5_spmd, body=%wide.region_0.4_spmd.sunk | while | flops 1345845504 | bytes 75555744 | solution.py:105
  119.2 1.6 gather_fusion
  120.8 1.6 gather_fusion.1
  122.3 1.9 fusion.79
  124.9 2.0 fusion.81
  128.7 3.0 fusion.84
  131.8 2.0 multiply_reduce_fusion.2
  135.6 1.5 fusion.83
  138.0 1.7 constant_dynamic-update-slice_fusion.7
  139.7 4.0 %bitcast_dynamic-update-slice_fusion.4 = f32[3,12,256,128]{3,1,2,0:T(8,128)} fusion(f32[3,12,256,128]{3,1,2,0:T(8,128)} %get-tuple-element.228, s32[]{:T(128)S(6)} %copy.106, f32[4,3,256,128]{3,2,1,0:T(8,128)S(1)} %fusion.83, s32[4,3]{0,1:T(4,128)S(1)} %copy.96), kind=kOutput, calls=%fused_computation.10.clone.1 | convolution fusion | flops 56623248 | bytes 3670068 | tf_op jit(solution)/shard_map/while/body/eval_jaxpr/anj,ankd->jkd/dot_general | solution.py:71
  143.7 4.0 %bitcast_dynamic-update-slice_fusion.5 = f32[3,12,256,128]{3,1,2,0:T(8,128)} fusion(f32[3,12,256,128]{3,1,2,0:T(8,128)} %get-tuple-element.229, s32[]{:T(128)S(6)} %copy.106, f32[4,3,256,128]{3,2,1,0:T(8,128)S(1)} %copy-done.1, s32[4,3]{0,1:T(4,128)S(1)} %copy.96), kind=kOutput, calls=%fused_computation.9.clone.1 | convolution fusion | flops 56623248 | bytes 3670068 | tf_op jit(solution)/shard_map/while/body/eval_jaxpr/anj,ankd->jkd/dot_general | solution.py:72
  150.1 1.6 gather_fusion
  151.6 1.6 gather_fusion.1
  153.2 1.9 fusion.79
  155.8 2.0 fusion.81
  159.6 3.0 fusion.84
  162.6 2.0 multiply_reduce_fusion.2
  168.9 1.7 constant_dynamic-update-slice_fusion.7
  170.5 4.0 %bitcast_dynamic-update-slice_fusion.4 = f32[3,12,256,128]{3,1,2,0:T(8,128)} fusion(f32[3,12,256,128]{3,1,2,0:T(8,128)} %get-tuple-element.228, s32[]{:T(128)S(6)} %copy.106, f32[4,3,256,128]{3,2,1,0:T(8,128)S(1)} %fusion.83, s32[4,3]{0,1:T(4,128)S(1)} %copy.96), kind=kOutput, calls=%fused_computation.10.clone.1 | convolution fusion | flops 56623248 | bytes 3670068 | tf_op jit(solution)/shard_map/while/body/eval_jaxpr/anj,ankd->jkd/dot_general | solution.py:71
  174.5 4.0 %bitcast_dynamic-update-slice_fusion.5 = f32[3,12,256,128]{3,1,2,0:T(8,128)} fusion(f32[3,12,256,128]{3,1,2,0:T(8,128)} %get-tuple-element.229, s32[]{:T(128)S(6)} %copy.106, f32[4,3,256,128]{3,2,1,0:T(8,128)S(1)} %copy-done.1, s32[4,3]{0,1:T(4,128)S(1)} %copy.96), kind=kOutput, calls=%fused_computation.9.clone.1 | convolution fusion | flops 56623248 | bytes 3670068 | tf_op jit(solution)/shard_map/while/body/eval_jaxpr/anj,ankd->jkd/dot_general | solution.py:72
  180.9 1.6 gather_fusion
  182.4 1.6 gather_fusion.1
  184.0 1.9 fusion.79
  186.6 2.0 fusion.81
  190.4 3.0 fusion.84
  193.4 2.0 multiply_reduce_fusion.2
  197.3 1.5 fusion.83
  199.7 1.7 constant_dynamic-update-slice_fusion.7
  201.3 4.0 %bitcast_dynamic-update-slice_fusion.4 = f32[3,12,256,128]{3,1,2,0:T(8,128)} fusion(f32[3,12,256,128]{3,1,2,0:T(8,128)} %get-tuple-element.228, s32[]{:T(128)S(6)} %copy.106, f32[4,3,256,128]{3,2,1,0:T(8,128)S(1)} %fusion.83, s32[4,3]{0,1:T(4,128)S(1)} %copy.96), kind=kOutput, calls=%fused_computation.10.clone.1 | convolution fusion | flops 56623248 | bytes 3670068 | tf_op jit(solution)/shard_map/while/body/eval_jaxpr/anj,ankd->jkd/dot_general | solution.py:71
  205.4 4.0 %bitcast_dynamic-update-slice_fusion.5 = f32[3,12,256,128]{3,1,2,0:T(8,128)} fusion(f32[3,12,256,128]{3,1,2,0:T(8,128)} %get-tuple-element.229, s32[]{:T(128)S(6)} %copy.106, f32[4,3,256,128]{3,2,1,0:T(8,128)S(1)} %copy-done.1, s32[4,3]{0,1:T(4,128)S(1)} %copy.96), kind=kOutput, calls=%fused_computation.9.clone.1 | convolution fusion | flops 56623248 | bytes 3670068 | tf_op jit(solution)/shard_map/while/body/eval_jaxpr/anj,ankd->jkd/dot_general | solution.py:72
  209.4 6.8 %copy.58 = f32[12,256,3,128]{1,0,3,2:T(8,128)} copy(f32[12,256,3,128]{3,0,1,2:T(8,128)} %bitcast.173) | data formatting | bytes 9437184 | tf_op jit(solution)/shard_map/transpose | solution.py:42
  216.2 6.9 %stack_reshape.7 = f32[1,3072,384]{1,2,0:T(8,128)} reshape(f32[12,256,3,128]{1,0,3,2:T(8,128)} %copy.58) | data formatting | bytes 9437184 | tf_op jit(solution)/shard_map/stack;reshape | solution.py:108
  223.0 6.7 %copy.57 = f32[12,256,3,128]{1,0,3,2:T(8,128)} copy(f32[12,256,3,128]{3,0,1,2:T(8,128)} %bitcast.174) | data formatting | bytes 9437184 | tf_op jit(solution)/shard_map/transpose | solution.py:42
  229.7 6.9 %stack_reshape.6 = f32[1,3072,384]{1,2,0:T(8,128)} reshape(f32[12,256,3,128]{1,0,3,2:T(8,128)} %copy.57) | data formatting | bytes 9437184 | tf_op jit(solution)/shard_map/stack;reshape | solution.py:108
  236.5 2.8 constant_dynamic-update-slice_fusion.3
  241.4 2.9 copy-done.2
  245.8 2.6 collective-permute-start.2
  249.7 14.7 %all_to_all.134 = bf16[4,256,384]{1,2,0:T(8,128)(2,1)S(1)} all-to-all(bf16[4,256,384]{1,2,0:T(8,128)(2,1)S(1)} %bitcast.184), channel_id=1, replica_groups=mesh['groups'=2,'seq'=4,'head'=4] {'head'}, dimensions={0} | all-to-all | bytes 1572864 | tf_op jit(solution)/shard_map/all_to_all | solution.py:115
  264.4 3.5 %all-to-all-start.5 = ((bf16[4,256,384]{1,2,0:T(8,128)(2,1)}), bf16[4,256,384]{1,2,0:T(8,128)(2,1)S(1)}, u32[]{:S(2)}, u32[]{:S(2)}) async-start(bf16[4,256,384]{1,2,0:T(8,128)(2,1)} %bitcast.183), calls=%async_computation.5 | async-start | bytes 1572864 | tf_op jit(solution)/shard_map/all_to_all | solution.py:116
  267.9 14.0 %collective-permute-done.2 = bf16[2,1024,384]{1,2,0:T(8,128)(2,1)} collective-permute-done((bf16[2,1024,384]{1,2,0:T(8,128)(2,1)}, bf16[2,1024,384]{1,2,0:T(8,128)(2,1)}, u32[]{:S(2)}, u32[]{:S(2)}) %collective-permute-start.2) | collective-permute-done | bytes 1572896 | tf_op jit(solution)/shard_map/ppermute | solution.py:30
  281.9 5.1 %collective-permute-done.3 = bf16[2,1024,384]{1,2,0:T(8,128)(2,1)} collective-permute-done((bf16[2,1024,384]{1,2,0:T(8,128)(2,1)S(1)}, bf16[2,1024,384]{1,2,0:T(8,128)(2,1)}, u32[]{:S(2)}, u32[]{:S(2)}) %collective-permute-start.3) | collective-permute-done | bytes 1572896 | tf_op jit(solution)/shard_map/ppermute | solution.py:30
  287.0 3.7 %fusion.35 = bf16[2,1024,384]{1,2,0:T(8,128)(2,1)S(1)} fusion(f32[2,3072,384]{1,2,0:T(8,128)} %copy-done.2, bf16[2,1024,384]{1,2,0:T(8,128)(2,1)} %collective-permute-done.3, bf16[2,1024,384]{1,2,0:T(8,128)(2,1)} %collective-permute-done.2), kind=kLoop, calls=%fused_computation.50 | loop fusion | flops 3932160 | bytes 7864320 | tf_op jit(solution)/shard_map/convert.1
  292.0 3.5 %all-to-all-start.7 = ((bf16[4,256,384]{2,1,0:T(8,128)(2,1)}), bf16[4,256,384]{2,1,0:T(8,128)(2,1)S(1)}, u32[]{:S(2)}, u32[]{:S(2)}) async-start(bf16[4,256,384]{2,1,0:T(8,128)(2,1)} %bitcast.55), calls=%async_computation.7 | async-start | bytes 1572864 | tf_op jit(solution)/shard_map/all_to_all | solution.py:120
  296.6 10.5 %all-to-all-done.7 = bf16[4,256,384]{2,1,0:T(8,128)(2,1)S(1)} async-done(((bf16[4,256,384]{2,1,0:T(8,128)(2,1)}), bf16[4,256,384]{2,1,0:T(8,128)(2,1)S(1)}, u32[]{:S(2)}, u32[]{:S(2)}) %all-to-all-start.7) | async-done | bytes 786464 | tf_op jit(solution)/shard_map/all_to_all | solution.py:120
  307.1 3.5 %all-to-all-start.6 = ((bf16[4,256,384]{2,1,0:T(8,128)(2,1)}), bf16[4,256,384]{2,1,0:T(8,128)(2,1)S(1)}, u32[]{:S(2)}, u32[]{:S(2)}) async-start(bf16[4,256,384]{2,1,0:T(8,128)(2,1)} %bitcast.52), calls=%async_computation.6 | async-start | bytes 1572864 | tf_op jit(solution)/shard_map/all_to_all | solution.py:117
  314.3 7.9 %all-to-all-done.6 = bf16[4,256,384]{2,1,0:T(8,128)(2,1)S(1)} async-done(((bf16[4,256,384]{2,1,0:T(8,128)(2,1)}), bf16[4,256,384]{2,1,0:T(8,128)(2,1)S(1)}, u32[]{:S(2)}, u32[]{:S(2)}) %all-to-all-start.6) | async-done | bytes 786464 | tf_op jit(solution)/shard_map/all_to_all | solution.py:117
  (117 shorter events, 43.7 us)
Async XLA Ops:
  0.6 5.9 %copy-start.8 = (bf16[256,1536]{1,0:T(8,128)(2,1)S(1)}, bf16[256,1536]{1,0:T(8,128)(2,1)}, u32[]{:S(2)}) copy-start(bf16[256,1536]{1,0:T(8,128)(2,1)} %param.10) | copy-start | bytes 2359300
  3.0 15.1 %all-to-all-start.1 = ((bf16[256,4,384]{0,2,1:T(8,128)(2,1)}), bf16[256,4,384]{0,2,1:T(8,128)(2,1)S(1)}, u32[]{:S(2)}, u32[]{:S(2)}) async-start(bf16[256,4,384]{0,2,1:T(8,128)(2,1)} %bitcast.30), calls=%async_computation.1 | async-start | bytes 1572864 | tf_op jit(solution)/shard_map/all_to_all | solution.py:82
  18.1 15.1 %all-to-all-start.2 = ((bf16[256,4,384]{0,2,1:T(8,128)(2,1)}), bf16[256,4,384]{0,2,1:T(8,128)(2,1)S(1)}, u32[]{:S(2)}, u32[]{:S(2)}) async-start(bf16[256,4,384]{0,2,1:T(8,128)(2,1)} %bitcast.33), calls=%async_computation.2 | async-start | bytes 1572864 | tf_op jit(solution)/shard_map/all_to_all | solution.py:83
  22.0 17.8 %copy-start.9 = (bf16[256,1536]{1,0:T(8,128)(2,1)S(1)}, bf16[256,1536]{1,0:T(8,128)(2,1)}, u32[]{:S(2)}) copy-start(bf16[256,1536]{1,0:T(8,128)(2,1)} %param.8) | copy-start | bytes 2359300
  33.6 10.9 %copy-start.12 = (s32[16,3]{0,1:T(4,128)S(1)}, s32[16,3]{0,1:T(4,128)}, u32[]{:S(2)}) copy-start(s32[16,3]{0,1:T(4,128)} %param.12) | copy-start | bytes 580
  33.6 10.9 %copy-start.13 = (s32[16,3]{0,1:T(4,128)S(1)}, s32[16,3]{0,1:T(4,128)}, u32[]{:S(2)}) copy-start(s32[16,3]{0,1:T(4,128)} %param.13) | copy-start | bytes 580
  33.6 11.1 %copy-start.10 = (bf16[256,1536]{1,0:T(8,128)(2,1)S(1)}, bf16[256,1536]{1,0:T(8,128)(2,1)}, u32[]{:S(2)}) copy-start(bf16[256,1536]{1,0:T(8,128)(2,1)} %param.11) | copy-start | bytes 2359300
  35.0 36.1 %collective-permute-start.1 = (bf16[2,1024,384]{2,1,0:T(8,128)(2,1)}, bf16[2,1024,384]{2,1,0:T(8,128)(2,1)}, u32[]{:S(2)}, u32[]{:S(2)}) collective-permute-start(bf16[2,1024,384]{2,1,0:T(8,128)(2,1)} %pad_maximum_fusion.1), channel_id=1, source_target_pairs={{4,0},{8,4},{12,8},{5,1},{9,5},{13,9},{6,2},{10,6},{14,10},{7,3},{... | collective-permute-start | bytes 4718600 | tf_op jit(solution)/shard_map/ppermute | solution.py:20
  38.5 37.9 %collective-permute-start = (bf16[2,1024,384]{2,1,0:T(8,128)(2,1)}, bf16[2,1024,384]{2,1,0:T(8,128)(2,1)}, u32[]{:S(2)}, u32[]{:S(2)}) collective-permute-start(bf16[2,1024,384]{2,1,0:T(8,128)(2,1)} %pad_maximum_fusion.1), channel_id=1, source_target_pairs={{0,4},{4,8},{8,12},{1,5},{5,9},{9,13},{2,6},{6,10},{10,14},{3,7},{... | collective-permute-start | bytes 4718600 | tf_op jit(solution)/shard_map/ppermute | solution.py:18
  40.9 40.1 %all-to-all-start = ((bf16[256,4,384]{0,2,1:T(8,128)(2,1)}), bf16[256,4,384]{0,2,1:T(8,128)(2,1)S(1)}, u32[]{:S(2)}, u32[]{:S(2)}) async-start(bf16[256,4,384]{0,2,1:T(8,128)(2,1)} %bitcast.26), calls=%async_computation | async-start | bytes 1572864 | tf_op jit(solution)/shard_map/all_to_all | solution.py:81
  81.0 35.9 %all-to-all-start.3 = ((bf16[256,4,384]{0,2,1:T(8,128)(2,1)}), bf16[256,4,384]{0,2,1:T(8,128)(2,1)}, u32[]{:S(2)}, u32[]{:S(2)}) async-start(bf16[256,4,384]{0,2,1:T(8,128)(2,1)} %bitcast.38), calls=%async_computation.3 | async-start | bytes 1572864 | tf_op jit(solution)/shard_map/all_to_all | solution.py:84
  116.8 0.9 copy-start.6
  122.3 2.6 copy-start.3
  128.7 3.0 copy-start.4
  133.7 1.1 copy-start
  137.1 6.5 %copy-start.1 = (f32[4,3,256,128]{3,2,1,0:T(8,128)S(1)}, f32[4,3,256,128]{3,2,1,0:T(8,128)}, u32[]{:S(2)}) copy-start(f32[4,3,256,128]{3,2,1,0:T(8,128)} %fusion.84) | copy-start | bytes 4718596 | tf_op jit(solution)/shard_map/while
  143.7 4.0 %copy-start.7 = (bf16[3,4,256,128]{2,3,0,1:T(8,128)(2,1)S(1)}, bf16[3,4,256,128]{2,3,0,1:T(8,128)(2,1)}, u32[]{:S(2)}) copy-start(bf16[3,4,256,128]{2,3,0,1:T(8,128)(2,1)} %copy-done.6) | copy-start | bytes 2359300 | tf_op jit(solution)/shard_map/while
  147.7 0.9 copy-start.6
  153.2 2.6 copy-start.3
  159.6 3.0 copy-start.4
  164.6 1.1 copy-start
  168.0 6.5 %copy-start.1 = (f32[4,3,256,128]{3,2,1,0:T(8,128)S(1)}, f32[4,3,256,128]{3,2,1,0:T(8,128)}, u32[]{:S(2)}) copy-start(f32[4,3,256,128]{3,2,1,0:T(8,128)} %fusion.84) | copy-start | bytes 4718596 | tf_op jit(solution)/shard_map/while
  174.5 4.0 %copy-start.7 = (bf16[3,4,256,128]{2,3,0,1:T(8,128)(2,1)S(1)}, bf16[3,4,256,128]{2,3,0,1:T(8,128)(2,1)}, u32[]{:S(2)}) copy-start(bf16[3,4,256,128]{2,3,0,1:T(8,128)(2,1)} %copy-done.6) | copy-start | bytes 2359300 | tf_op jit(solution)/shard_map/while
  178.5 0.9 copy-start.6
  184.0 2.6 copy-start.3
  190.4 3.0 copy-start.4
  195.4 1.1 copy-start
  198.8 6.6 %copy-start.1 = (f32[4,3,256,128]{3,2,1,0:T(8,128)S(1)}, f32[4,3,256,128]{3,2,1,0:T(8,128)}, u32[]{:S(2)}) copy-start(f32[4,3,256,128]{3,2,1,0:T(8,128)} %fusion.84) | copy-start | bytes 4718596 | tf_op jit(solution)/shard_map/while
  205.4 4.0 %copy-start.7 = (bf16[3,4,256,128]{2,3,0,1:T(8,128)(2,1)S(1)}, bf16[3,4,256,128]{2,3,0,1:T(8,128)(2,1)}, u32[]{:S(2)}) copy-start(bf16[3,4,256,128]{2,3,0,1:T(8,128)(2,1)} %copy-done.6) | copy-start | bytes 2359300 | tf_op jit(solution)/shard_map/while
  236.5 3.8 %copy-start.5 = (f32[1,3072,384]{1,2,0:T(8,128)S(1)}, f32[1,3072,384]{1,2,0:T(8,128)}, u32[]{:S(2)}) copy-start(f32[1,3072,384]{1,2,0:T(8,128)} %stack_reshape.7) | copy-start | bytes 14155780
  240.6 3.7 %copy-start.2 = (f32[2,3072,384]{1,2,0:T(8,128)}, f32[2,3072,384]{1,2,0:T(8,128)S(1)}, u32[]{:S(2)}) copy-start(f32[2,3072,384]{1,2,0:T(8,128)S(1)} %constant_dynamic-update-slice_fusion.2) | copy-start | bytes 28311556
  244.3 5.4 %copy-start.11 = (bf16[3,4,256,128]{2,3,0,1:T(8,128)(2,1)S(1)}, bf16[3,4,256,128]{2,3,0,1:T(8,128)(2,1)}, u32[]{:S(2)}) copy-start(bf16[3,4,256,128]{2,3,0,1:T(8,128)(2,1)} %get-tuple-element.64) | copy-start | bytes 2359300
  245.8 36.1 %collective-permute-start.2 = (bf16[2,1024,384]{1,2,0:T(8,128)(2,1)}, bf16[2,1024,384]{1,2,0:T(8,128)(2,1)}, u32[]{:S(2)}, u32[]{:S(2)}) collective-permute-start(bf16[2,1024,384]{1,2,0:T(8,128)(2,1)} %get-tuple-element.126), channel_id=1, source_target_pairs={{4,0},{8,4},{12,8},{5,1},{9,5},{13,9},{6,2},{10,6},{14,10},{7,3},{... | collective-permute-start | bytes 4718600 | tf_op jit(solution)/shard_map/ppermute | solution.py:30
  248.4 38.6 %collective-permute-start.3 = (bf16[2,1024,384]{1,2,0:T(8,128)(2,1)S(1)}, bf16[2,1024,384]{1,2,0:T(8,128)(2,1)}, u32[]{:S(2)}, u32[]{:S(2)}) collective-permute-start(bf16[2,1024,384]{1,2,0:T(8,128)(2,1)S(1)} %get-tuple-element.127), channel_id=1, source_target_pairs={{0,4},{4,8},{8,12},{1,5},{5,9},{9,13},{2,6},{6,10},{10,14},{3,7},{... | collective-permute-start | bytes 4718600 | tf_op jit(solution)/shard_map/ppermute | solution.py:30
  264.4 27.6 %all-to-all-start.5 = ((bf16[4,256,384]{1,2,0:T(8,128)(2,1)}), bf16[4,256,384]{1,2,0:T(8,128)(2,1)S(1)}, u32[]{:S(2)}, u32[]{:S(2)}) async-start(bf16[4,256,384]{1,2,0:T(8,128)(2,1)} %bitcast.183), calls=%async_computation.5 | async-start | bytes 1572864 | tf_op jit(solution)/shard_map/all_to_all | solution.py:116
  292.0 15.1 %all-to-all-start.7 = ((bf16[4,256,384]{2,1,0:T(8,128)(2,1)}), bf16[4,256,384]{2,1,0:T(8,128)(2,1)S(1)}, u32[]{:S(2)}, u32[]{:S(2)}) async-start(bf16[4,256,384]{2,1,0:T(8,128)(2,1)} %bitcast.55), calls=%async_computation.7 | async-start | bytes 1572864 | tf_op jit(solution)/shard_map/all_to_all | solution.py:120
  307.1 15.1 %all-to-all-start.6 = ((bf16[4,256,384]{2,1,0:T(8,128)(2,1)}), bf16[4,256,384]{2,1,0:T(8,128)(2,1)S(1)}, u32[]{:S(2)}, u32[]{:S(2)}) async-start(bf16[4,256,384]{2,1,0:T(8,128)(2,1)} %bitcast.52), calls=%async_computation.6 | async-start | bytes 1572864 | tf_op jit(solution)/shard_map/all_to_all | solution.py:117
where the time goes:
time: 326 us; the launch traced here: 324 us
  local copies, waits for them, and re-layouts  111 us (34%)
  waiting for transfers between devices  89.5 us (27%)
  matrix products  57.4 us (18%)
  starting transfers between devices  33.8 us (10%)
  other arithmetic  15.9 us (5%)
  blocking collectives  14.7 us (5%)
    ppermute x1, waiting for transfers between devices, extended_2(): lax.ppermute(head, axis, [((i + 1) % count, i) for i in range(ends)])  25.2 us
    ppermute x2, waiting for transfers between devices, shifted(): lax.ppermute(value, axis, [(source, source + steps) for source in range(i...  19.1 us
    unnamed x27, local copies, waits for them, and re-layouts  17.3 us
    all_to_all x1, blocking collectives, body(): lax.all_to_all(head_join(attended), 'head', split_axis=0, concat_axis=1,...  14.7 us
    another operation x3, local copies, waits for them, and re-layouts, body(): grads = jnp.stack([head_join(key_sums), head_join(value_sums)])  14 us
    transpose x2, local copies, waits for them, and re-layouts, head_join(): blocks.transpose(1, 2, 0, 3).reshape(tiles * tile_size, heads * head_size)  13.5 us
    dynamic_update_slice x12, local copies, waits for them, and re-layouts, body(): lax.map(with_partials, (q_heads, g_heads, k_heads, v_heads))  13 us
    dot_general x3, matrix products, forward_head(): jnp.einsum('anj,ankd->jkd', onehot, value_slots, precision=lax.Precision....  12.1 us
  transfers between devices with their start and end apart: 11, of which 8 were waited for; matrix products, arithmetic and copies ran while one was open for 16% of the time, Pallas kernels for 0%

commit v1 on v0

--- a/solution.py
+++ b/solution.py
@@ -5,6 +5,22 @@
 
 HEADS = 12
 HEAD_DIM = 128
+
+
+def exchange_in_pairs(x, axis, split, join):
+    ways, here = (lax.axis_size(axis), lax.axis_index(axis))
+    width = x.shape[split] // ways
+    shape = list(x.shape)
+    shape[split] = width
+    height = shape[join]
+    shape[join] = height * ways
+    full = jnp.zeros(shape, x.dtype)
+    for mask in range(ways):
+        part = lax.dynamic_slice_in_dim(x, (here ^ mask) * width, width, axis=split)
+        if mask:
+            part = lax.ppermute(part, axis, [(d, d ^ mask) for d in range(ways)])
+        full = lax.dynamic_update_slice_in_dim(full, part, (here ^ mask) * height, axis=join)
+    return full
 
 
 def extended_2(cells, sides, width):
@@ -80,7 +96,7 @@
     queries, keys, values, out_grads = (
         lax.all_to_all(query, "head", split_axis=1, concat_axis=0, tiled=True),
         lax.all_to_all(key_in, "head", split_axis=1, concat_axis=0, tiled=True),
-        lax.all_to_all(value, "head", split_axis=1, concat_axis=0, tiled=True),
+        exchange_in_pairs(value, "head", 1, 0),
         lax.all_to_all(grad_out, "head", split_axis=1, concat_axis=0, tiled=True),
     )
     tile_size = queries.shape[0] // members

time: 326 us -> 310 us (0.951)
  local copies, waits for them, and re-layouts: 111 us -> 102 us
  waiting for transfers between devices: 89.5 us -> 83.8 us
    ppermute x0 -> x3, waiting for transfers between devices: none -> 17.1 us  [exchange_in_pairs(): part = lax.ppermute(part, axis, [(d, d ^ mask) for d in range(ways)])]
    all_to_all x1 -> x0, waiting for transfers between devices: 11.2 us -> none  [body(): lax.all_to_all(value, 'head', split_axis=1, concat_axis=0, tiled=True)]
    all_to_all x1, waiting for transfers between devices: 10.5 us -> 0.01 us  [body(): lax.all_to_all(key_in, 'head', split_axis=1, concat_axis=0, tiled=True)]
    slice x2 -> x1, local copies, waits for them, and re-layouts: 8.53 us -> 4.1 us  [body(): v_heads = head_split(extended[1], 3 * members, heads)]
    all_to_all x1 -> x0, starting transfers between devices: 3.49 us -> none  [body(): lax.all_to_all(value, 'head', split_axis=1, concat_axis=0, tiled=True)]
    unnamed x27 -> x24, local copies, waits for them, and re-layouts: 17.3 us -> 16.4 us
  transfers between devices with their start and end apart: 11 -> 13, of which waited for: 8 -> 8; matrix products, arithmetic and copies ran while one was open for 16% -> 13% of each run, Pallas kernels for 0% -> 0%
where the time goes in v1:
time: 310 us; the launch traced here: 308 us
  local copies, waits for them, and re-layouts  102 us (33%)
  waiting for transfers between devices  83.8 us (27%)
  matrix products  57.4 us (19%)
  starting transfers between devices  32.6 us (11%)
  other arithmetic  15.8 us (5%)
  blocking collectives  14.7 us (5%)
    ppermute x1, waiting for transfers between devices, extended_2(): lax.ppermute(head, axis, [((i + 1) % count, i) for i in range(ends)])  24 us
    ppermute x2, waiting for transfers between devices, shifted(): lax.ppermute(value, axis, [(source, source + steps) for source in range(i...  19.1 us
    ppermute x3, waiting for transfers between devices, exchange_in_pairs(): part = lax.ppermute(part, axis, [(d, d ^ mask) for d in range(ways)])  17.1 us
    unnamed x24, local copies, waits for them, and re-layouts  16.4 us
    all_to_all x1, blocking collectives, body(): lax.all_to_all(head_join(attended), 'head', split_axis=0, concat_axis=1,...  14.7 us
    another operation x3, local copies, waits for them, and re-layouts, body(): grads = jnp.stack([head_join(key_sums), head_join(value_sums)])  14 us
    transpose x2, local copies, waits for them, and re-layouts, head_join(): blocks.transpose(1, 2, 0, 3).reshape(tiles * tile_size, heads * head_size)  13.5 us
    dynamic_update_slice x12, local copies, waits for them, and re-layouts, body(): lax.map(with_partials, (q_heads, g_heads, k_heads, v_heads))  13 us
  transfers between devices with their start and end apart: 13, of which 8 were waited for; matrix products, arithmetic and copies ran while one was open for 13% of the time, Pallas kernels for 0%

profile of v1, /device:TPU:24, one launch (start us, length us, event | category | flops | bytes accessed | tf_op | source)
XLA Modules:
  0.0 307.7 jit_solution(5636474915138768471)
XLA Ops:
  0.6 1.5 copy.106
  3.3 3.5 %all-to-all-start.1 = ((bf16[256,4,384]{2,0,1:T(8,128)(2,1)}), bf16[256,4,384]{2,0,1:T(8,128)(2,1)S(1)}, u32[]{:S(2)}, u32[]{:S(2)}) async-start(bf16[256,4,384]{2,0,1:T(8,128)(2,1)} %copy.107), calls=%async_computation.1 | async-start | bytes 1572864 | tf_op jit(solution)/shard_map/all_to_all | solution.py:98
  6.9 1.8 collective-permute-start.2
  9.4 12.7 %collective-permute-done.2 = bf16[256,384]{1,0:T(8,128)(2,1)S(1)} collective-permute-done((bf16[256,384]{1,0:T(8,128)(2,1)S(1)}, bf16[256,384]{1,0:T(8,128)(2,1)S(1)}, u32[]{:S(2)}, u32[]{:S(2)}) %collective-permute-start.2) | collective-permute-done | bytes 196640 | tf_op jit(solution)/shard_map/ppermute | solution.py:21
  22.4 4.4 %collective-permute-done.1 = bf16[256,384]{1,0:T(8,128)(2,1)S(1)} collective-permute-done((bf16[256,384]{1,0:T(8,128)(2,1)S(1)}, bf16[256,384]{1,0:T(8,128)(2,1)S(1)}, u32[]{:S(2)}, u32[]{:S(2)}) %collective-permute-start.1) | collective-permute-done | bytes 196640 | tf_op jit(solution)/shard_map/ppermute | solution.py:21
  28.7 3.5 %collective-permute-start.4 = (bf16[2,1024,384]{1,2,0:T(8,128)(2,1)}, bf16[2,1024,384]{1,2,0:T(8,128)(2,1)}, u32[]{:S(2)}, u32[]{:S(2)}) collective-permute-start(bf16[2,1024,384]{1,2,0:T(8,128)(2,1)} %pad_maximum_fusion.1), channel_id=1, source_target_pairs={{4,0},{8,4},{12,8},{5,1},{9,5},{13,9},{6,2},{10,6},{14,10},{7,3},{... | collective-permute-start | bytes 4718600 | tf_op jit(solution)/shard_map/ppermute | solution.py:36
  34.6 3.5 %all-to-all-start = ((bf16[256,4,384]{0,2,1:T(8,128)(2,1)}), bf16[256,4,384]{0,2,1:T(8,128)(2,1)S(1)}, u32[]{:S(2)}, u32[]{:S(2)}) async-start(bf16[256,4,384]{0,2,1:T(8,128)(2,1)} %bitcast.26), calls=%async_computation | async-start | bytes 1572864 | tf_op jit(solution)/shard_map/all_to_all | solution.py:97
  38.4 2.3 copy.114
  40.7 24.0 %collective-permute-done.4 = bf16[2,1024,384]{1,2,0:T(8,128)(2,1)} collective-permute-done((bf16[2,1024,384]{1,2,0:T(8,128)(2,1)}, bf16[2,1024,384]{1,2,0:T(8,128)(2,1)}, u32[]{:S(2)}, u32[]{:S(2)}) %collective-permute-start.4) | collective-permute-done | bytes 1572896 | tf_op jit(solution)/shard_map/ppermute | solution.py:36
  64.8 5.2 %collective-permute-done.3 = bf16[2,1024,384]{1,2,0:T(8,128)(2,1)} collective-permute-done((bf16[2,1024,384]{1,2,0:T(8,128)(2,1)}, bf16[2,1024,384]{1,2,0:T(8,128)(2,1)}, u32[]{:S(2)}, u32[]{:S(2)}) %collective-permute-start.3) | collective-permute-done | bytes 1572896 | tf_op jit(solution)/shard_map/ppermute | solution.py:34
  70.0 4.6 %pad_maximum_fusion = bf16[2,3072,384]{1,2,0:T(8,128)(2,1)} fusion(bf16[2,1024,384]{1,2,0:T(8,128)(2,1)} %collective-permute-done.4, bf16[1,1024,384]{1,2,0:T(8,128)(2,1)S(1)} %constant_dynamic-update-slice_fusion.4, bf16[1,1024,384]{1,2,0:T(8,128)(2,1)S(1)} %copy.112, bf16[2,1024,384]{1,2,0:T(8,128)(2,1)} %collective-permute-done.3), kind=kLoop, calls=%fused_computation.47 | loop fusion | flops 18874368 | bytes 9437184 | tf_op jit(solution)/shard_map/concatenate | solution.py:32
  74.6 4.2 %all-to-all-start.2 = ((bf16[256,4,384]{0,2,1:T(8,128)(2,1)}), bf16[256,4,384]{0,2,1:T(8,128)(2,1)}, u32[]{:S(2)}, u32[]{:S(2)}) async-start(bf16[256,4,384]{0,2,1:T(8,128)(2,1)} %bitcast.39), calls=%async_computation.2 | async-start | bytes 1572864 | tf_op jit(solution)/shard_map/all_to_all | solution.py:100
  78.8 4.1 %fusion.37 = (bf16[1,3072,384]{1,2,0:T(8,128)(2,1)}, bf16[1,3072,384]{1,2,0:T(8,128)(2,1)S(1)}) fusion(bf16[2,3072,384]{1,2,0:T(8,128)(2,1)} %pad_maximum_fusion), kind=kLoop, calls=%fused_computation.67 | loop fusion | bytes 9437184 | tf_op jit(solution)/shard_map/slice | solution.py:114
  82.9 5.4 %reshape_squeeze.7 = bf16[12,256,3,128]{1,0,3,2:T(8,128)(2,1)} reshape(bf16[1,3072,384]{1,2,0:T(8,128)(2,1)} %get-tuple-element.158) | data formatting | bytes 4718592 | tf_op jit(solution)/shard_map/reshape;squeeze | solution.py:51
  88.3 4.8 %copy.117 = bf16[3,12,256,128]{3,2,1,0:T(8,128)(2,1)} copy(bf16[3,12,256,128]{2,1,3,0:T(8,128)(2,1)} %bitcast.170) | data formatting | bytes 4718592 | tf_op jit(solution)/shard_map/while | solution.py:121
  93.1 3.0 reshape_squeeze.6
  96.1 4.8 %copy.116 = bf16[3,12,256,128]{3,2,1,0:T(8,128)(2,1)} copy(bf16[3,12,256,128]{2,1,3,0:T(8,128)(2,1)} %bitcast.171) | data formatting | bytes 4718592 | tf_op jit(solution)/shard_map/while | solution.py:121
  100.9 92.5 %while.16 = (s32[]{:T(128)}, bf16[3,4,256,128]{2,3,0,1:T(8,128)(2,1)}, bf16[3,4,256,128]{2,3,0,1:T(8,128)(2,1)}, f32[3,12,256,128]{3,1,2,0:T(8,128)}, f32[3,12,2...) while((s32[]{:T(128)}, ...), condition=%wide.region_4.5_spmd, body=%wide.region_0.4_spmd.sunk | while | flops 1345845504 | bytes 75555744 | solution.py:121
  103.3 1.6 gather_fusion
  104.8 1.6 gather_fusion.1
  106.4 1.9 fusion.79
  108.9 2.0 fusion.81
  112.8 3.0 fusion.84
  115.8 2.0 multiply_reduce_fusion.2
  119.6 1.5 fusion.83
  122.0 1.7 constant_dynamic-update-slice_fusion.11
  123.7 4.0 %bitcast_dynamic-update-slice_fusion.4 = f32[3,12,256,128]{3,1,2,0:T(8,128)} fusion(f32[3,12,256,128]{3,1,2,0:T(8,128)} %get-tuple-element.262, s32[]{:T(128)S(6)} %copy.174, f32[4,3,256,128]{3,2,1,0:T(8,128)S(1)} %fusion.83, s32[4,3]{0,1:T(4,128)S(1)} %copy.160), kind=kOutput, calls=%fused_computation.10.clone.1 | convolution fusion | flops 56623248 | bytes 3670068 | tf_op jit(solution)/shard_map/while/body/eval_jaxpr/anj,ankd->jkd/dot_general | solution.py:87
  127.7 4.0 %bitcast_dynamic-update-slice_fusion.5 = f32[3,12,256,128]{3,1,2,0:T(8,128)} fusion(f32[3,12,256,128]{3,1,2,0:T(8,128)} %get-tuple-element.263, s32[]{:T(128)S(6)} %copy.174, f32[4,3,256,128]{3,2,1,0:T(8,128)S(1)} %copy-done.1, s32[4,3]{0,1:T(4,128)S(1)} %copy.160), kind=kOutput, calls=%fused_computation.9.clone.1 | convolution fusion | flops 56623248 | bytes 3670068 | tf_op jit(solution)/shard_map/while/body/eval_jaxpr/anj,ankd->jkd/dot_general | solution.py:88
  134.1 1.6 gather_fusion
  135.7 1.6 gather_fusion.1
  137.2 1.9 fusion.79
  139.8 2.0 fusion.81
  143.6 3.0 fusion.84
  146.7 2.0 multiply_reduce_fusion.2
  150.5 1.5 fusion.83
  152.9 1.7 constant_dynamic-update-slice_fusion.11
  154.6 4.0 %bitcast_dynamic-update-slice_fusion.4 = f32[3,12,256,128]{3,1,2,0:T(8,128)} fusion(f32[3,12,256,128]{3,1,2,0:T(8,128)} %get-tuple-element.262, s32[]{:T(128)S(6)} %copy.174, f32[4,3,256,128]{3,2,1,0:T(8,128)S(1)} %fusion.83, s32[4,3]{0,1:T(4,128)S(1)} %copy.160), kind=kOutput, calls=%fused_computation.10.clone.1 | convolution fusion | flops 56623248 | bytes 3670068 | tf_op jit(solution)/shard_map/while/body/eval_jaxpr/anj,ankd->jkd/dot_general | solution.py:87
  158.6 4.0 %bitcast_dynamic-update-slice_fusion.5 = f32[3,12,256,128]{3,1,2,0:T(8,128)} fusion(f32[3,12,256,128]{3,1,2,0:T(8,128)} %get-tuple-element.263, s32[]{:T(128)S(6)} %copy.174, f32[4,3,256,128]{3,2,1,0:T(8,128)S(1)} %copy-done.1, s32[4,3]{0,1:T(4,128)S(1)} %copy.160), kind=kOutput, calls=%fused_computation.9.clone.1 | convolution fusion | flops 56623248 | bytes 3670068 | tf_op jit(solution)/shard_map/while/body/eval_jaxpr/anj,ankd->jkd/dot_general | solution.py:88
  164.9 1.6 gather_fusion
  166.5 1.6 gather_fusion.1
  168.1 1.9 fusion.79
  170.6 2.0 fusion.81
  174.4 3.0 fusion.84
  177.5 2.0 multiply_reduce_fusion.2
  181.3 1.5 fusion.83
  183.7 1.7 constant_dynamic-update-slice_fusion.11
  185.4 4.0 %bitcast_dynamic-update-slice_fusion.4 = f32[3,12,256,128]{3,1,2,0:T(8,128)} fusion(f32[3,12,256,128]{3,1,2,0:T(8,128)} %get-tuple-element.262, s32[]{:T(128)S(6)} %copy.174, f32[4,3,256,128]{3,2,1,0:T(8,128)S(1)} %fusion.83, s32[4,3]{0,1:T(4,128)S(1)} %copy.160), kind=kOutput, calls=%fused_computation.10.clone.1 | convolution fusion | flops 56623248 | bytes 3670068 | tf_op jit(solution)/shard_map/while/body/eval_jaxpr/anj,ankd->jkd/dot_general | solution.py:87
  189.4 4.0 %bitcast_dynamic-update-slice_fusion.5 = f32[3,12,256,128]{3,1,2,0:T(8,128)} fusion(f32[3,12,256,128]{3,1,2,0:T(8,128)} %get-tuple-element.263, s32[]{:T(128)S(6)} %copy.174, f32[4,3,256,128]{3,2,1,0:T(8,128)S(1)} %copy-done.1, s32[4,3]{0,1:T(4,128)S(1)} %copy.160), kind=kOutput, calls=%fused_computation.9.clone.1 | convolution fusion | flops 56623248 | bytes 3670068 | tf_op jit(solution)/shard_map/while/body/eval_jaxpr/anj,ankd->jkd/dot_general | solution.py:88
  193.4 6.8 %copy.122 = f32[12,256,3,128]{1,0,3,2:T(8,128)} copy(f32[12,256,3,128]{3,0,1,2:T(8,128)} %bitcast.172) | data formatting | bytes 9437184 | tf_op jit(solution)/shard_map/transpose | solution.py:58
  200.2 6.9 %stack_reshape.7 = f32[1,3072,384]{1,2,0:T(8,128)} reshape(f32[12,256,3,128]{1,0,3,2:T(8,128)} %copy.122) | data formatting | bytes 9437184 | tf_op jit(solution)/shard_map/stack;reshape | solution.py:124
  207.1 6.7 %copy.121 = f32[12,256,3,128]{1,0,3,2:T(8,128)} copy(f32[12,256,3,128]{3,0,1,2:T(8,128)} %bitcast.173) | data formatting | bytes 9437184 | tf_op jit(solution)/shard_map/transpose | solution.py:58
  213.7 6.9 %stack_reshape.6 = f32[1,3072,384]{1,2,0:T(8,128)} reshape(f32[12,256,3,128]{1,0,3,2:T(8,128)} %copy.121) | data formatting | bytes 9437184 | tf_op jit(solution)/shard_map/stack;reshape | solution.py:124
  220.6 2.8 constant_dynamic-update-slice_fusion.3
  225.4 2.9 copy-done.2
  229.8 2.6 collective-permute-start.5
  233.7 14.7 %all_to_all.118 = bf16[4,256,384]{1,2,0:T(8,128)(2,1)S(1)} all-to-all(bf16[4,256,384]{1,2,0:T(8,128)(2,1)S(1)} %bitcast.183), channel_id=1, replica_groups=mesh['groups'=2,'seq'=4,'head'=4] {'head'}, dimensions={0} | all-to-all | bytes 1572864 | tf_op jit(solution)/shard_map/all_to_all | solution.py:131
  248.4 3.5 %all-to-all-start.4 = ((bf16[4,256,384]{1,2,0:T(8,128)(2,1)}), bf16[4,256,384]{1,2,0:T(8,128)(2,1)S(1)}, u32[]{:S(2)}, u32[]{:S(2)}) async-start(bf16[4,256,384]{1,2,0:T(8,128)(2,1)} %bitcast.182), calls=%async_computation.4 | async-start | bytes 1572864 | tf_op jit(solution)/shard_map/all_to_all | solution.py:132
  251.9 14.0 %collective-permute-done.5 = bf16[2,1024,384]{1,2,0:T(8,128)(2,1)} collective-permute-done((bf16[2,1024,384]{1,2,0:T(8,128)(2,1)}, bf16[2,1024,384]{1,2,0:T(8,128)(2,1)}, u32[]{:S(2)}, u32[]{:S(2)}) %collective-permute-start.5) | collective-permute-done | bytes 1572896 | tf_op jit(solution)/shard_map/ppermute | solution.py:46
  265.9 5.1 %collective-permute-done.6 = bf16[2,1024,384]{1,2,0:T(8,128)(2,1)} collective-permute-done((bf16[2,1024,384]{1,2,0:T(8,128)(2,1)S(1)}, bf16[2,1024,384]{1,2,0:T(8,128)(2,1)}, u32[]{:S(2)}, u32[]{:S(2)}) %collective-permute-start.6) | collective-permute-done | bytes 1572896 | tf_op jit(solution)/shard_map/ppermute | solution.py:46
  271.0 3.7 %fusion.35 = bf16[2,1024,384]{1,2,0:T(8,128)(2,1)S(1)} fusion(f32[2,3072,384]{1,2,0:T(8,128)} %copy-done.2, bf16[2,1024,384]{1,2,0:T(8,128)(2,1)} %collective-permute-done.6, bf16[2,1024,384]{1,2,0:T(8,128)(2,1)} %collective-permute-done.5), kind=kLoop, calls=%fused_computation.50 | loop fusion | flops 3932160 | bytes 7864320 | tf_op jit(solution)/shard_map/convert.1
  276.0 3.5 %all-to-all-start.6 = ((bf16[4,256,384]{2,1,0:T(8,128)(2,1)}), bf16[4,256,384]{2,1,0:T(8,128)(2,1)S(1)}, u32[]{:S(2)}, u32[]{:S(2)}) async-start(bf16[4,256,384]{2,1,0:T(8,128)(2,1)} %bitcast.56), calls=%async_computation.6 | async-start | bytes 1572864 | tf_op jit(solution)/shard_map/all_to_all | solution.py:136
  280.7 10.5 %all-to-all-done.6 = bf16[4,256,384]{2,1,0:T(8,128)(2,1)S(1)} async-done(((bf16[4,256,384]{2,1,0:T(8,128)(2,1)}), bf16[4,256,384]{2,1,0:T(8,128)(2,1)S(1)}, u32[]{:S(2)}, u32[]{:S(2)}) %all-to-all-start.6) | async-done | bytes 786464 | tf_op jit(solution)/shard_map/all_to_all | solution.py:136
  291.1 3.5 %all-to-all-start.5 = ((bf16[4,256,384]{2,1,0:T(8,128)(2,1)}), bf16[4,256,384]{2,1,0:T(8,128)(2,1)S(1)}, u32[]{:S(2)}, u32[]{:S(2)}) async-start(bf16[4,256,384]{2,1,0:T(8,128)(2,1)} %bitcast.53), calls=%async_computation.5 | async-start | bytes 1572864 | tf_op jit(solution)/shard_map/all_to_all | solution.py:133
  298.4 7.9 %all-to-all-done.5 = bf16[4,256,384]{2,1,0:T(8,128)(2,1)S(1)} async-done(((bf16[4,256,384]{2,1,0:T(8,128)(2,1)}), bf16[4,256,384]{2,1,0:T(8,128)(2,1)S(1)}, u32[]{:S(2)}, u32[]{:S(2)}) %all-to-all-start.5) | async-done | bytes 786464 | tf_op jit(solution)/shard_map/all_to_all | solution.py:133
  (126 shorter events, 41.8 us)
Async XLA Ops:
  0.6 6.2 %copy-start.8 = (bf16[256,1536]{1,0:T(8,128)(2,1)S(1)}, bf16[256,1536]{1,0:T(8,128)(2,1)}, u32[]{:S(2)}) copy-start(bf16[256,1536]{1,0:T(8,128)(2,1)} %param.10) | copy-start | bytes 2359300
  3.3 23.8 %all-to-all-start.1 = ((bf16[256,4,384]{2,0,1:T(8,128)(2,1)}), bf16[256,4,384]{2,0,1:T(8,128)(2,1)S(1)}, u32[]{:S(2)}, u32[]{:S(2)}) async-start(bf16[256,4,384]{2,0,1:T(8,128)(2,1)} %copy.107), calls=%async_computation.1 | async-start | bytes 1572864 | tf_op jit(solution)/shard_map/all_to_all | solution.py:98
  6.9 15.2 %collective-permute-start.2 = (bf16[256,384]{1,0:T(8,128)(2,1)S(1)}, bf16[256,384]{1,0:T(8,128)(2,1)S(1)}, u32[]{:S(2)}, u32[]{:S(2)}) collective-permute-start(bf16[256,384]{1,0:T(8,128)(2,1)S(1)} %get-tuple-element.162), channel_id=1, source_target_pairs={{0,3},{1,2},{2,1},{3,0},{4,7},{5,6},{6,5},{7,4},{8,11},{9,10},{10,... | collective-permute-start | bytes 589832 | tf_op jit(solution)/shard_map/ppermute | solution.py:21
  8.7 13.6 %collective-permute-start = (bf16[256,384]{1,0:T(8,128)(2,1)S(1)}, bf16[256,384]{1,0:T(8,128)(2,1)S(1)}, u32[]{:S(2)}, u32[]{:S(2)}) collective-permute-start(bf16[256,384]{1,0:T(8,128)(2,1)S(1)} %get-tuple-element.163), channel_id=1, source_target_pairs={{0,1},{1,0},{2,3},{3,2},{4,5},{5,4},{6,7},{7,6},{8,9},{9,8},{10,11... | collective-permute-start | bytes 589832 | tf_op jit(solution)/shard_map/ppermute | solution.py:21
  9.0 17.8 %collective-permute-start.1 = (bf16[256,384]{1,0:T(8,128)(2,1)S(1)}, bf16[256,384]{1,0:T(8,128)(2,1)S(1)}, u32[]{:S(2)}, u32[]{:S(2)}) collective-permute-start(bf16[256,384]{1,0:T(8,128)(2,1)S(1)} %get-tuple-element.165), channel_id=1, source_target_pairs={{0,2},{1,3},{2,0},{3,1},{4,6},{5,7},{6,4},{7,5},{8,10},{9,11},{10,... | collective-permute-start | bytes 589832 | tf_op jit(solution)/shard_map/ppermute | solution.py:21
  26.8 6.6 %copy-start.9 = (bf16[256,1536]{1,0:T(8,128)(2,1)S(1)}, bf16[256,1536]{1,0:T(8,128)(2,1)}, u32[]{:S(2)}) copy-start(bf16[256,1536]{1,0:T(8,128)(2,1)} %param.8) | copy-start | bytes 2359300
  27.4 10.8 %copy-start.11 = (s32[16,3]{0,1:T(4,128)S(1)}, s32[16,3]{0,1:T(4,128)}, u32[]{:S(2)}) copy-start(s32[16,3]{0,1:T(4,128)} %param.12) | copy-start | bytes 580
  27.4 10.8 %copy-start.12 = (s32[16,3]{0,1:T(4,128)S(1)}, s32[16,3]{0,1:T(4,128)}, u32[]{:S(2)}) copy-start(s32[16,3]{0,1:T(4,128)} %param.13) | copy-start | bytes 580
  28.7 36.1 %collective-permute-start.4 = (bf16[2,1024,384]{1,2,0:T(8,128)(2,1)}, bf16[2,1024,384]{1,2,0:T(8,128)(2,1)}, u32[]{:S(2)}, u32[]{:S(2)}) collective-permute-start(bf16[2,1024,384]{1,2,0:T(8,128)(2,1)} %pad_maximum_fusion.1), channel_id=1, source_target_pairs={{4,0},{8,4},{12,8},{5,1},{9,5},{13,9},{6,2},{10,6},{14,10},{7,3},{... | collective-permute-start | bytes 4718600 | tf_op jit(solution)/shard_map/ppermute | solution.py:36
  32.2 37.9 %collective-permute-start.3 = (bf16[2,1024,384]{1,2,0:T(8,128)(2,1)}, bf16[2,1024,384]{1,2,0:T(8,128)(2,1)}, u32[]{:S(2)}, u32[]{:S(2)}) collective-permute-start(bf16[2,1024,384]{1,2,0:T(8,128)(2,1)} %pad_maximum_fusion.1), channel_id=1, source_target_pairs={{0,4},{4,8},{8,12},{1,5},{5,9},{9,13},{2,6},{6,10},{10,14},{3,7},{... | collective-permute-start | bytes 4718600 | tf_op jit(solution)/shard_map/ppermute | solution.py:34
  34.6 40.0 %all-to-all-start = ((bf16[256,4,384]{0,2,1:T(8,128)(2,1)}), bf16[256,4,384]{0,2,1:T(8,128)(2,1)S(1)}, u32[]{:S(2)}, u32[]{:S(2)}) async-start(bf16[256,4,384]{0,2,1:T(8,128)(2,1)} %bitcast.26), calls=%async_computation | async-start | bytes 1572864 | tf_op jit(solution)/shard_map/all_to_all | solution.py:97
  74.6 26.3 %all-to-all-start.2 = ((bf16[256,4,384]{0,2,1:T(8,128)(2,1)}), bf16[256,4,384]{0,2,1:T(8,128)(2,1)}, u32[]{:S(2)}, u32[]{:S(2)}) async-start(bf16[256,4,384]{0,2,1:T(8,128)(2,1)} %bitcast.39), calls=%async_computation.2 | async-start | bytes 1572864 | tf_op jit(solution)/shard_map/all_to_all | solution.py:100
  100.9 0.9 copy-start.6
  106.4 2.6 copy-start.3
  112.7 3.0 copy-start.4
  117.8 1.1 copy-start
  121.2 6.5 %copy-start.1 = (f32[4,3,256,128]{3,2,1,0:T(8,128)S(1)}, f32[4,3,256,128]{3,2,1,0:T(8,128)}, u32[]{:S(2)}) copy-start(f32[4,3,256,128]{3,2,1,0:T(8,128)} %fusion.84) | copy-start | bytes 4718596 | tf_op jit(solution)/shard_map/while
  127.7 4.1 %copy-start.7 = (bf16[3,4,256,128]{2,3,0,1:T(8,128)(2,1)S(1)}, bf16[3,4,256,128]{2,3,0,1:T(8,128)(2,1)}, u32[]{:S(2)}) copy-start(bf16[3,4,256,128]{2,3,0,1:T(8,128)(2,1)} %copy-done.6) | copy-start | bytes 2359300 | tf_op jit(solution)/shard_map/while
  131.8 0.9 copy-start.6
  137.2 2.6 copy-start.3
  143.6 3.0 copy-start.4
  148.7 1.1 copy-start
  152.1 6.5 %copy-start.1 = (f32[4,3,256,128]{3,2,1,0:T(8,128)S(1)}, f32[4,3,256,128]{3,2,1,0:T(8,128)}, u32[]{:S(2)}) copy-start(f32[4,3,256,128]{3,2,1,0:T(8,128)} %fusion.84) | copy-start | bytes 4718596 | tf_op jit(solution)/shard_map/while
  158.6 4.0 %copy-start.7 = (bf16[3,4,256,128]{2,3,0,1:T(8,128)(2,1)S(1)}, bf16[3,4,256,128]{2,3,0,1:T(8,128)(2,1)}, u32[]{:S(2)}) copy-start(bf16[3,4,256,128]{2,3,0,1:T(8,128)(2,1)} %copy-done.6) | copy-start | bytes 2359300 | tf_op jit(solution)/shard_map/while
  162.6 0.9 copy-start.6
  168.0 2.6 copy-start.3
  174.4 3.0 copy-start.4
  179.5 1.1 copy-start
  182.9 6.5 %copy-start.1 = (f32[4,3,256,128]{3,2,1,0:T(8,128)S(1)}, f32[4,3,256,128]{3,2,1,0:T(8,128)}, u32[]{:S(2)}) copy-start(f32[4,3,256,128]{3,2,1,0:T(8,128)} %fusion.84) | copy-start | bytes 4718596 | tf_op jit(solution)/shard_map/while
  189.4 4.0 %copy-start.7 = (bf16[3,4,256,128]{2,3,0,1:T(8,128)(2,1)S(1)}, bf16[3,4,256,128]{2,3,0,1:T(8,128)(2,1)}, u32[]{:S(2)}) copy-start(bf16[3,4,256,128]{2,3,0,1:T(8,128)(2,1)} %copy-done.6) | copy-start | bytes 2359300 | tf_op jit(solution)/shard_map/while
  220.6 3.8 %copy-start.5 = (f32[1,3072,384]{1,2,0:T(8,128)S(1)}, f32[1,3072,384]{1,2,0:T(8,128)}, u32[]{:S(2)}) copy-start(f32[1,3072,384]{1,2,0:T(8,128)} %stack_reshape.7) | copy-start | bytes 14155780
  224.7 3.7 %copy-start.2 = (f32[2,3072,384]{1,2,0:T(8,128)}, f32[2,3072,384]{1,2,0:T(8,128)S(1)}, u32[]{:S(2)}) copy-start(f32[2,3072,384]{1,2,0:T(8,128)S(1)} %constant_dynamic-update-slice_fusion.2) | copy-start | bytes 28311556
  228.3 5.4 %copy-start.10 = (bf16[3,4,256,128]{2,3,0,1:T(8,128)(2,1)S(1)}, bf16[3,4,256,128]{2,3,0,1:T(8,128)(2,1)}, u32[]{:S(2)}) copy-start(bf16[3,4,256,128]{2,3,0,1:T(8,128)(2,1)} %get-tuple-element.64) | copy-start | bytes 2359300
  229.8 36.1 %collective-permute-start.5 = (bf16[2,1024,384]{1,2,0:T(8,128)(2,1)}, bf16[2,1024,384]{1,2,0:T(8,128)(2,1)}, u32[]{:S(2)}, u32[]{:S(2)}) collective-permute-start(bf16[2,1024,384]{1,2,0:T(8,128)(2,1)} %get-tuple-element.156), channel_id=1, source_target_pairs={{4,0},{8,4},{12,8},{5,1},{9,5},{13,9},{6,2},{10,6},{14,10},{7,3},{... | collective-permute-start | bytes 4718600 | tf_op jit(solution)/shard_map/ppermute | solution.py:46
  232.4 38.6 %collective-permute-start.6 = (bf16[2,1024,384]{1,2,0:T(8,128)(2,1)S(1)}, bf16[2,1024,384]{1,2,0:T(8,128)(2,1)}, u32[]{:S(2)}, u32[]{:S(2)}) collective-permute-start(bf16[2,1024,384]{1,2,0:T(8,128)(2,1)S(1)} %get-tuple-element.157), channel_id=1, source_target_pairs={{0,4},{4,8},{8,12},{1,5},{5,9},{9,13},{2,6},{6,10},{10,14},{3,7},{... | collective-permute-start | bytes 4718600 | tf_op jit(solution)/shard_map/ppermute | solution.py:46
  248.4 27.6 %all-to-all-start.4 = ((bf16[4,256,384]{1,2,0:T(8,128)(2,1)}), bf16[4,256,384]{1,2,0:T(8,128)(2,1)S(1)}, u32[]{:S(2)}, u32[]{:S(2)}) async-start(bf16[4,256,384]{1,2,0:T(8,128)(2,1)} %bitcast.182), calls=%async_computation.4 | async-start | bytes 1572864 | tf_op jit(solution)/shard_map/all_to_all | solution.py:132
  276.0 15.1 %all-to-all-start.6 = ((bf16[4,256,384]{2,1,0:T(8,128)(2,1)}), bf16[4,256,384]{2,1,0:T(8,128)(2,1)S(1)}, u32[]{:S(2)}, u32[]{:S(2)}) async-start(bf16[4,256,384]{2,1,0:T(8,128)(2,1)} %bitcast.56), calls=%async_computation.6 | async-start | bytes 1572864 | tf_op jit(solution)/shard_map/all_to_all | solution.py:136
  291.1 15.1 %all-to-all-start.5 = ((bf16[4,256,384]{2,1,0:T(8,128)(2,1)}), bf16[4,256,384]{2,1,0:T(8,128)(2,1)S(1)}, u32[]{:S(2)}, u32[]{:S(2)}) async-start(bf16[4,256,384]{2,1,0:T(8,128)(2,1)} %bitcast.53), calls=%async_computation.5 | async-start | bytes 1572864 | tf_op jit(solution)/shard_map/all_to_all | solution.py:133
